TPU v7x, 32 devices: a whole 2x2x4 slice. The times are simulated.
32 devices in a mesh: frame: 4 (over y, x), head: 8 (over z, core).
Axes of the slice: x: 2, y: 2, z: 4, core: 2. Of those that a mesh axis runs over, the one named last changes fastest.
Arguments:
- tokens: float32 [8, 1024, 1024], P('frame', 'head'), may hold values from -48 to 48
- qkv_weight: float32 [1024, 3072], replicated
- out_weight: float32 [1024, 1024], replicated, may hold values from -0.1875 to 0.1875
- norm_gain: float32 [1024], replicated, may hold values from 0.1 to 1.9
- proj_weight: float32 [1024, 256], replicated, may hold values from -0.1875 to 0.1875
- up_weight: bfloat16 [256, 4096], replicated, may hold values from -0.375 to 0.375
- conv_weight: bfloat16 [2, 3, 3, 256, 256], replicated, may hold values from -0.125 to 0.125
- conv_bias: float32 [2, 256], replicated, may hold values from -3 to 3
- block_lists: int32 [64, 13], P('frame'), may hold values from 0 to 63, as said below
- block_counts: int32 [64], P('frame'), may hold values from 1 to 13, as said below
Outputs:
- refined: bfloat16 [8, 128, 128, 256], P('frame', 'head')
Inputs may be any that keep to these rules, and one draw needn't show every extreme that they name: `block_lists`: row b names 13 different key blocks and its first entry is block b itself; entries at or after the row's count are padding and are ignored. `block_counts`: some query block in every draw has all 13 entries valid.
All inputs are finite; a program needn't handle non-finite values.
Results may differ from a plain program's by a relative error of at most 0.0057.
Values may be sent and summed in bfloat16 or wider, within the bound.
A program may use at most 128 MiB of HBM per device.

v0:
```python
import math

import jax
import jax.numpy as jnp
from jax import lax
from jax.sharding import PartitionSpec as P

HEADS = 16
GRID = 32
BLOCK = 128


highest = lax.Precision.HIGHEST
eps_norm = 1e-05


def extended_2(block, sides, width):
    for axis, dim in sides:
        count = lax.axis_size(axis)
        forward = [(i, i + 1) for i in range(count - 1)]
        backward = [(target, source) for source, target in forward]
        low = lax.ppermute(
            lax.slice_in_dim(block, block.shape[dim] - width, None, axis=dim), axis, forward
        )
        high = lax.ppermute(lax.slice_in_dim(block, 0, width, axis=dim), axis, backward)
        block = jnp.concatenate([low, block, high], axis=dim)
    return block


def attend_padded(queries, key_values, block_ids, counts, factor):
    groups, slot_total = block_ids.shape
    block_size = queries.shape[1]
    half = queries.shape[3] // 2
    picked = key_values[block_ids]
    picked = picked.reshape((groups, slot_total * block_size) + picked.shape[3:])
    scores = jnp.einsum("gihe,gjhe->ghij", queries, picked, precision=highest) * factor
    slot_of = jnp.arange(slot_total * block_size, dtype=jnp.int32) // block_size
    usable = slot_of[None, :] < counts[:, None]
    scores = jnp.where(usable[:, None, None, :], scores, -jnp.inf)
    row_max = jnp.max(scores, axis=3, keepdims=True)
    weights = jnp.exp(scores - row_max)
    totals = jnp.sum(weights, axis=3)
    blended = jnp.einsum("ghij,gjhe->gihe", weights, picked, precision=highest)
    return blended[:, :, :, half:] / jnp.transpose(totals, (0, 2, 1))[:, :, :, None]


def layer_norm(rows, gain):
    centre = jnp.mean(rows, axis=-1, keepdims=True)
    centred = rows - centre
    spread = jnp.mean(centred * centred, axis=-1, keepdims=True)
    return centred * lax.rsqrt(spread + eps_norm) * gain


def conv_window(padded, weight):
    frames_here, rows_in, cols_in, channels = padded.shape
    rows_out = rows_in - 2
    cols_out = cols_in - 2
    summed = jnp.zeros((frames_here * rows_out * cols_out, weight.shape[-1]), jnp.float32)
    for row_off in range(3):
        for col_off in range(3):
            window = padded[:, row_off : row_off + rows_out, col_off : col_off + cols_out, :]
            summed = summed + jnp.dot(
                window.reshape(-1, channels),
                weight[row_off, col_off],
                preferred_element_type=jnp.float32,
            )
    return summed.reshape(frames_here, rows_out, cols_out, -1)


def pad_columns(image):
    return jnp.pad(image, ((0, 0), (0, 0), (1, 1), (0, 0)))


def on_device(
    tokens,
    qkv_weight,
    out_weight,
    norm_gain,
    proj_weight,
    up_weight,
    conv_weight,
    conv_bias,
    block_lists,
    block_counts,
):
    local_frames, strip_tokens, model_width = tokens.shape
    head_groups = lax.axis_size("head")
    local_heads = HEADS // head_groups
    head_dim = model_width // HEADS
    column_width = local_heads * 3 * head_dim
    frame_tokens = strip_tokens * head_groups
    flat_strip = tokens.reshape(-1, model_width)
    columns = lax.dynamic_slice_in_dim(
        qkv_weight, lax.axis_index("head") * column_width, column_width, 1
    )
    piece = lax.all_gather(tokens, "head", axis=1, tiled=True)
    rows_flat = piece.reshape(-1, model_width)
    result = jnp.dot(rows_flat, columns, precision=highest, preferred_element_type=jnp.float32)
    packed = result.reshape(piece.shape[0], piece.shape[1], column_width)
    local_rows = local_frames * frame_tokens
    packed = packed.reshape(local_rows, local_heads, 3 * head_dim)
    query_mask = (jnp.arange(2 * head_dim, dtype=jnp.int32) < head_dim).astype(jnp.float32)
    queries = (packed[:, :, : 2 * head_dim] * query_mask).reshape(
        -1, BLOCK, local_heads, 2 * head_dim
    )
    own_pairs = packed[:, :, head_dim:].reshape(local_rows, local_heads * 2 * head_dim)
    all_pairs = lax.all_gather(own_pairs, "frame", axis=0, tiled=True)
    all_pairs = all_pairs.reshape(-1, BLOCK, local_heads, 2 * head_dim)
    local_blocks = queries.shape[0]
    group_blocks = math.gcd(local_blocks, max(1, 512 // BLOCK))
    group_count = local_blocks // group_blocks
    factor = head_dim ** (-0.5)
    grouped = (
        queries.reshape(group_count, group_blocks, BLOCK, local_heads, 2 * head_dim),
        block_lists.reshape(group_count, group_blocks, -1),
        block_counts.reshape(group_count, group_blocks),
    )

    def one_group(items):
        return attend_padded(items[0], all_pairs, items[1], items[2], factor)

    attended = lax.map(one_group, grouped)
    attended = attended.reshape(local_frames, head_groups, strip_tokens, local_heads * head_dim)
    attended = lax.all_to_all(attended, "head", split_axis=1, concat_axis=3, tiled=True)
    attended = attended.reshape(-1, model_width)
    stream = flat_strip + jnp.dot(
        attended, out_weight, precision=highest, preferred_element_type=jnp.float32
    )
    normed = layer_norm(stream, norm_gain)
    features = jnp.dot(
        normed, proj_weight, precision=highest, preferred_element_type=jnp.float32
    ).astype(jnp.bfloat16)
    channels = features.shape[1]
    strip_rows = strip_tokens // GRID
    lifted = jnp.dot(features, up_weight, preferred_element_type=jnp.float32).astype(jnp.bfloat16)
    lifted = lifted.reshape(local_frames, strip_rows, GRID, 4, 4, channels)
    upsampled = jnp.transpose(lifted, (0, 1, 3, 2, 4, 5)).reshape(
        local_frames, 4 * strip_rows, 4 * GRID, channels
    )
    activated = jnp.maximum(upsampled, jnp.zeros((), jnp.bfloat16))
    rimmed = extended_2(activated, (("head", 1),), 1)
    first_conv = conv_window(pad_columns(rimmed), conv_weight[0]) + conv_bias[0]
    hidden = jnp.maximum(first_conv, 0.0).astype(jnp.bfloat16)
    extended = extended_2(hidden, (("head", 1),), 1)
    second = conv_window(pad_columns(extended), conv_weight[1]) + conv_bias[1]
    return (upsampled.astype(jnp.float32) + second).astype(jnp.bfloat16)


def solution(mesh):
    in_specs = (
        P("frame", "head", None),
        P(),
        P(),
        P(),
        P(),
        P(),
        P(),
        P(),
        P("frame", None),
        P("frame"),
    )
    out_specs = P("frame", "head", None, None)
    return jax.shard_map(
        on_device, mesh=mesh, in_specs=in_specs, out_specs=out_specs, check_vma=False
    )
```

profile of v0, /device:TPU:1, one launch (start us, length us, event | category | flops | bytes accessed | tf_op | source)
XLA Modules:
  0.0 552.0 jit_solution(14968831860393375033)
XLA Ops:
  7.3 86.2 %all-gather.3.cloned.1.call-done = f32[2,1024,1024]{2,1,0:T(8,128)} async-done(((f32[2,128,1024]{2,1,0:T(8,128)}), f32[2,1024,1024]{2,1,0:T(8,128)}) %all-gather.3.cloned.1.call-update) | async-done | bytes 8388624 | tf_op jit(solution)/shard_map/all_gather | solution.py:96
  93.5 22.6 %fusion.26 = f32[384,2048]{1,0:T(8,128)S(1)} fusion(f32[2048,1024]{1,0:T(8,128)} %bitcast.179, f32[1024,3072]{1,0:T(8,128)} %param.13, s32[]{:T(128)S(6)} %select_n.35), kind=kOutput, calls=%fused_computation.69 | convolution fusion | flops 9663676416 | bytes 13107204 | tf_op jit(solution)/shard_map/dot_general | solution.py:98
  128.2 78.9 %all-gather.5.cloned.1.call-done = f32[8192,256]{1,0:T(8,128)} async-done(((f32[2048,256]{1,0:T(8,128)}), f32[8192,256]{1,0:T(8,128)}) %all-gather.5.cloned.1.call-update) | async-done | bytes 8388624 | tf_op jit(solution)/shard_map/all_gather | solution.py:107
  207.1 10.9 %reshape.206 = f32[64,128,2,128]{3,2,1,0:T(2,128)} reshape(f32[8192,256]{1,0:T(8,128)} %all-gather.5.cloned.1.call-done) | data formatting | bytes 16777216 | tf_op jit(solution)/shard_map/reshape | solution.py:108
  218.0 185.1 %while.12 = (s32[]{:T(128)}, f32[4,4,128,2,64]{2,4,3,1,0:T(8,128)S(1)}, s32[4,4,13]{2,1,0:T(4,128)}, f32[64,128,2,128]{3,2,1,0:T(2,128)}, s32[4,4]{1,0:T(4,128)S(1)}, /*index=5*/f32[4,4,128,2,128]{4,2,1,0,3:T(8,128)}, s32[]{:T(128)}) while((s32[]{:T(128)}, f32[4,4,128,2,64]{2,4,3,1,0:T(8,128)S(1)}, s32[4,4,13]{2,1,0:T(4,128)}, ...), condition=%wide.region_3.4_spmd, body=%wide.region_0.3_spmd.sunk | while | flops 5251615744 | bytes 90243968 | solution.py:122
  219.1 14.1 %gather_fusion = f32[52,128,2,128]{3,2,1,0:T(2,128)} fusion(f32[64,128,2,128]{3,2,1,0:T(2,128)} %get-tuple-element.210, s32[1024]{0:T(1024)S(1)} %pad_clamp_fusion.2), kind=kCustom, calls=%fused_computation.clone.1 | custom fusion | bytes 13631696 | tf_op jit(solution)/shard_map/while/body/eval_jaxpr/gather | solution.py:34
  233.2 11.1 %copy.95 = f32[4,1664,2,128]{1,3,2,0:T(8,128)} copy(f32[4,1664,2,128]{3,2,1,0:T(2,128)} %bitcast.165) | data formatting | bytes 13631488 | tf_op jit(solution)/shard_map/while/body/eval_jaxpr/reshape | solution.py:35
  244.4 9.0 %fusion.82 = (f32[4,2,128]{2,1,0:T(2,128)S(1)}, f32[4,2,128,1664]{3,2,1,0:T(8,128)S(1)}) fusion(pred[4,1664]{1,0:T(4,128)(4,1)S(1)} %broadcast_compare_fusion.2, f32[4,1664,2,128]{1,3,2,0:T(8,128)} %copy.95, f32[4,4,128,2,128]{4,2,1,0,3:T(8,128)} %get-tuple-element.212, s32[]{:T(128)} %get-tuple-element.200), kind=kOutput, calls=%fused_computation.3.clone.1 | convolution fusion | flops 2622356480 | bytes 14167040 | tf_op jit(solution)/shard_map/while/body/eval_jaxpr/gihe,gjhe->ghij/dot_general | solution.py:36
  256.4 8.0 %fusion.83 = f32[4,128,2,128]{1,3,2,0:T(8,128)S(1)} fusion(f32[4,1664,2,128]{1,3,2,0:T(8,128)S(1)} %copy-done.2, f32[4,2,128,1664]{3,2,1,0:T(8,128)S(1)} %get-tuple-element.191, f32[4,2,128]{2,1,0:T(2,128)S(1)} %get-tuple-element.192, pred[4,1664]{1,0:T(4,128)(4,1)S(1)} %broadcast_compare_fusion.2), kind=kOutput, calls=%fused_computation.10.clone.1 | convolution fusion | flops 2622357504 | bytes 14166528 | tf_op jit(solution)/shard_map/while/body/eval_jaxpr/ghij,gjhe->gihe/dot_general | solution.py:43
  265.2 14.2 %gather_fusion = f32[52,128,2,128]{3,2,1,0:T(2,128)} fusion(f32[64,128,2,128]{3,2,1,0:T(2,128)} %get-tuple-element.210, s32[1024]{0:T(1024)S(1)} %pad_clamp_fusion.2), kind=kCustom, calls=%fused_computation.clone.1 | custom fusion | bytes 13631696 | tf_op jit(solution)/shard_map/while/body/eval_jaxpr/gather | solution.py:34
  279.4 11.1 %copy.95 = f32[4,1664,2,128]{1,3,2,0:T(8,128)} copy(f32[4,1664,2,128]{3,2,1,0:T(2,128)} %bitcast.165) | data formatting | bytes 13631488 | tf_op jit(solution)/shard_map/while/body/eval_jaxpr/reshape | solution.py:35
  290.6 9.0 %fusion.82 = (f32[4,2,128]{2,1,0:T(2,128)S(1)}, f32[4,2,128,1664]{3,2,1,0:T(8,128)S(1)}) fusion(pred[4,1664]{1,0:T(4,128)(4,1)S(1)} %broadcast_compare_fusion.2, f32[4,1664,2,128]{1,3,2,0:T(8,128)} %copy.95, f32[4,4,128,2,128]{4,2,1,0,3:T(8,128)} %get-tuple-element.212, s32[]{:T(128)} %get-tuple-element.200), kind=kOutput, calls=%fused_computation.3.clone.1 | convolution fusion | flops 2622356480 | bytes 14167040 | tf_op jit(solution)/shard_map/while/body/eval_jaxpr/gihe,gjhe->ghij/dot_general | solution.py:36
  302.5 8.0 %fusion.83 = f32[4,128,2,128]{1,3,2,0:T(8,128)S(1)} fusion(f32[4,1664,2,128]{1,3,2,0:T(8,128)S(1)} %copy-done.2, f32[4,2,128,1664]{3,2,1,0:T(8,128)S(1)} %get-tuple-element.191, f32[4,2,128]{2,1,0:T(2,128)S(1)} %get-tuple-element.192, pred[4,1664]{1,0:T(4,128)(4,1)S(1)} %broadcast_compare_fusion.2), kind=kOutput, calls=%fused_computation.10.clone.1 | convolution fusion | flops 2622357504 | bytes 14166528 | tf_op jit(solution)/shard_map/while/body/eval_jaxpr/ghij,gjhe->gihe/dot_general | solution.py:43
  311.4 14.2 %gather_fusion = f32[52,128,2,128]{3,2,1,0:T(2,128)} fusion(f32[64,128,2,128]{3,2,1,0:T(2,128)} %get-tuple-element.210, s32[1024]{0:T(1024)S(1)} %pad_clamp_fusion.2), kind=kCustom, calls=%fused_computation.clone.1 | custom fusion | bytes 13631696 | tf_op jit(solution)/shard_map/while/body/eval_jaxpr/gather | solution.py:34
  325.6 11.1 %copy.95 = f32[4,1664,2,128]{1,3,2,0:T(8,128)} copy(f32[4,1664,2,128]{3,2,1,0:T(2,128)} %bitcast.165) | data formatting | bytes 13631488 | tf_op jit(solution)/shard_map/while/body/eval_jaxpr/reshape | solution.py:35
  336.7 9.0 %fusion.82 = (f32[4,2,128]{2,1,0:T(2,128)S(1)}, f32[4,2,128,1664]{3,2,1,0:T(8,128)S(1)}) fusion(pred[4,1664]{1,0:T(4,128)(4,1)S(1)} %broadcast_compare_fusion.2, f32[4,1664,2,128]{1,3,2,0:T(8,128)} %copy.95, f32[4,4,128,2,128]{4,2,1,0,3:T(8,128)} %get-tuple-element.212, s32[]{:T(128)} %get-tuple-element.200), kind=kOutput, calls=%fused_computation.3.clone.1 | convolution fusion | flops 2622356480 | bytes 14167040 | tf_op jit(solution)/shard_map/while/body/eval_jaxpr/gihe,gjhe->ghij/dot_general | solution.py:36
  348.7 8.0 %fusion.83 = f32[4,128,2,128]{1,3,2,0:T(8,128)S(1)} fusion(f32[4,1664,2,128]{1,3,2,0:T(8,128)S(1)} %copy-done.2, f32[4,2,128,1664]{3,2,1,0:T(8,128)S(1)} %get-tuple-element.191, f32[4,2,128]{2,1,0:T(2,128)S(1)} %get-tuple-element.192, pred[4,1664]{1,0:T(4,128)(4,1)S(1)} %broadcast_compare_fusion.2), kind=kOutput, calls=%fused_computation.10.clone.1 | convolution fusion | flops 2622357504 | bytes 14166528 | tf_op jit(solution)/shard_map/while/body/eval_jaxpr/ghij,gjhe->gihe/dot_general | solution.py:43
  357.6 14.2 %gather_fusion = f32[52,128,2,128]{3,2,1,0:T(2,128)} fusion(f32[64,128,2,128]{3,2,1,0:T(2,128)} %get-tuple-element.210, s32[1024]{0:T(1024)S(1)} %pad_clamp_fusion.2), kind=kCustom, calls=%fused_computation.clone.1 | custom fusion | bytes 13631696 | tf_op jit(solution)/shard_map/while/body/eval_jaxpr/gather | solution.py:34
  371.7 11.1 %copy.95 = f32[4,1664,2,128]{1,3,2,0:T(8,128)} copy(f32[4,1664,2,128]{3,2,1,0:T(2,128)} %bitcast.165) | data formatting | bytes 13631488 | tf_op jit(solution)/shard_map/while/body/eval_jaxpr/reshape | solution.py:35
  382.9 9.0 %fusion.82 = (f32[4,2,128]{2,1,0:T(2,128)S(1)}, f32[4,2,128,1664]{3,2,1,0:T(8,128)S(1)}) fusion(pred[4,1664]{1,0:T(4,128)(4,1)S(1)} %broadcast_compare_fusion.2, f32[4,1664,2,128]{1,3,2,0:T(8,128)} %copy.95, f32[4,4,128,2,128]{4,2,1,0,3:T(8,128)} %get-tuple-element.212, s32[]{:T(128)} %get-tuple-element.200), kind=kOutput, calls=%fused_computation.3.clone.1 | convolution fusion | flops 2622356480 | bytes 14167040 | tf_op jit(solution)/shard_map/while/body/eval_jaxpr/gihe,gjhe->ghij/dot_general | solution.py:36
  394.9 8.0 %fusion.83 = f32[4,128,2,128]{1,3,2,0:T(8,128)S(1)} fusion(f32[4,1664,2,128]{1,3,2,0:T(8,128)S(1)} %copy-done.2, f32[4,2,128,1664]{3,2,1,0:T(8,128)S(1)} %get-tuple-element.191, f32[4,2,128]{2,1,0:T(2,128)S(1)} %get-tuple-element.192, pred[4,1664]{1,0:T(4,128)(4,1)S(1)} %broadcast_compare_fusion.2), kind=kOutput, calls=%fused_computation.10.clone.1 | convolution fusion | flops 2622357504 | bytes 14166528 | tf_op jit(solution)/shard_map/while/body/eval_jaxpr/ghij,gjhe->gihe/dot_general | solution.py:43
  404.4 5.4 all-to-all-start
  412.7 22.9 %all-to-all-done = f32[2,8,128,128]{3,2,0,1:T(8,128)} async-done(((f32[2,8,128,128]{3,2,0,1:T(8,128)}), f32[2,8,128,128]{3,2,0,1:T(8,128)}, u32[]{:S(2)}, u32[]{:S(2)}) %all-to-all-start) | async-done | bytes 1048608 | tf_op jit(solution)/shard_map/all_to_all | solution.py:124
  437.5 6.2 %fusion.47 = (f32[256]{0:T(256)S(1)}, f32[256,1024]{1,0:T(8,128)S(1)}) fusion(f32[256,1024]{1,0:T(8,128)S(1)} %bitcast.194, f32[1024,1024]{1,0:T(8,128)} %param.14, f32[32,8,8,128]{3,2,1,0:T(8,128)S(1)} %bitcast.195), kind=kOutput, calls=%fused_computation.118 | convolution fusion | flops 3221749504 | bytes 7341056 | tf_op jit(solution)/shard_map/dot_general | solution.py:126
  447.9 4.5 max.34
  452.4 5.0 copy.67
  469.3 5.8 %pad_maximum_fusion.2 = (bf16[2,16,128,256]{3,0,2,1:T(2,128)(2,1)S(1)}, bf16[2,16,128,256]{3,0,2,1:T(2,128)(2,1)S(1)}) fusion(bf16[2,1,128,256]{3,0,2,1:T(2,128)(2,1)S(1)} %collective-permute-done.1, bf16[2,16,128,256]{3,0,2,1:T(2,128)(2,1)S(1)} %bitcast.168, bf16[2,1,128,256]{3,0,2,1:T(2,128)(2,1)S(1)} %collective-permute-done), kind=kLoop, calls=%fused_computation.64 | loop fusion | flops 2097152 | bytes 6553600 | tf_op jit(solution)/shard_map/concatenate | solution.py:26
  479.7 10.9 %fusion.43 = (bf16[2,16,128,256]{3,0,2,1:T(2,128)(2,1)S(1)}, bf16[2,16,128,256]{3,0,2,1:T(2,128)(2,1)S(1)}, bf16[2,16,128,256]{3,0,2,1:T(2,128)(2,1)S(1)}, bf16[...) fusion(bf16[2,18,130,256]{3,0,2,1:T(2,128)(2,1)S(1)} %select_maxim, ...), kind=kLoop, calls=%fused_computation.114 | loop fusion | bytes 25165824 | tf_op jit(solution)/shard_map/slice | solution.py:61
  509.5 6.4 %reshape.229 = f32[2,4,32,4,4,256]{5,4,3,2,1,0:T(4,128)} reshape(bf16[256,4096]{1,0:T(8,128)(2,1)} %get-tuple-element.151) | data formatting | bytes 6291456 | tf_op jit(solution)/shard_map/convert_element_type | solution.py:146
  515.9 5.3 copy.65
  521.1 5.4 reshape.228
  527.6 5.2 fusion.42
  (129 shorter events, 86.6 us)
Async XLA Ops:
  6.5 438.6 %copy-start = (bf16[256,4096]{1,0:T(8,128)(2,1)S(1)}, bf16[256,4096]{1,0:T(8,128)(2,1)}, u32[]{:S(2)}) copy-start(bf16[256,4096]{1,0:T(8,128)(2,1)} %param.17) | copy-start | bytes 6291460
  6.5 86.9 %all-gather.3.cloned.1.call-start = ((), (), s32[]{:S(2)}) async-start(), calls=%async_computation.1 | async-start | bytes 9437184 | tf_op jit(solution)/shard_map/all_gather | solution.py:96
  7.3 199.8 %all-gather.5.cloned.1.call-start = ((), (), s32[]{:S(2)}) async-start(), calls=%async_computation.2 | async-start | bytes 10485760 | tf_op jit(solution)/shard_map/all_gather | solution.py:107
  121.5 0.7 copy-start.13
  253.4 2.9 copy-start.2
  299.6 2.9 copy-start.2
  345.8 2.9 copy-start.2
  391.9 2.9 copy-start.2
  404.4 31.1 %all-to-all-start = ((f32[2,8,128,128]{3,2,0,1:T(8,128)}), f32[2,8,128,128]{3,2,0,1:T(8,128)}, u32[]{:S(2)}, u32[]{:S(2)}) async-start(f32[2,8,128,128]{3,2,0,1:T(8,128)} %copy.63), calls=%async_computation | async-start | bytes 2097152 | tf_op jit(solution)/shard_map/all_to_all | solution.py:124
  435.6 1.9 copy-start.9
  437.5 6.5 %copy-start.10 = (f32[1024,256]{1,0:T(8,128)S(1)}, f32[1024,256]{1,0:T(8,128)}, u32[]{:S(2)}) copy-start(f32[1024,256]{1,0:T(8,128)} %param.16) | copy-start | bytes 3145732
  437.5 6.5 %copy-start.11 = (f32[1024]{0:T(1024)S(1)}, f32[1024]{0:T(1024)}, u32[]{:S(2)}) copy-start(f32[1024]{0:T(1024)} %param.15) | copy-start | bytes 12292
  452.4 10.2 %copy-start.12 = (f32[2,256]{1,0:T(2,128)S(1)}, f32[2,256]{1,0:T(2,128)}, u32[]{:S(2)}) copy-start(f32[2,256]{1,0:T(2,128)} %param.19) | copy-start | bytes 6148
  452.4 10.2 %copy-start.5 = (bf16[2,4,32,4,4,256]{5,4,3,2,1,0:T(4,128)(2,1)S(1)}, bf16[2,4,32,4,4,256]{5,4,3,2,1,0:T(4,128)(2,1)}, u32[]{:S(2)}) copy-start(bf16[2,4,32,4,4,256]{5,4,3,2,1,0:T(4,128)(2,1)} %max.34) | copy-start | bytes 6291460
  458.3 11.0 %collective-permute-start = (bf16[2,1,128,256]{3,0,2,1:T(2,128)(2,1)}, bf16[2,1,128,256]{3,0,2,1:T(2,128)(2,1)S(1)}, u32[]{:S(2)}, u32[]{:S(2)}) collective-permute-start(bf16[2,1,128,256]{3,0,2,1:T(2,128)(2,1)} %get-tuple-element.144), channel_id=1, source_target_pairs={{0,1},{1,2},{2,3},{3,4},{4,5},{5,6},{6,7},{8,9},{9,10},{10,11},{11... | collective-permute-start | bytes 393224 | tf_op jit(solution)/shard_map/ppermute | solution.py:22
  460.2 9.1 %collective-permute-start.1 = (bf16[2,1,128,256]{3,0,2,1:T(2,128)(2,1)}, bf16[2,1,128,256]{3,0,2,1:T(2,128)(2,1)S(1)}, u32[]{:S(2)}, u32[]{:S(2)}) collective-permute-start(bf16[2,1,128,256]{3,0,2,1:T(2,128)(2,1)} %get-tuple-element.145), channel_id=1, source_target_pairs={{1,0},{2,1},{3,2},{4,3},{5,4},{6,5},{7,6},{9,8},{10,9},{11,10},{12... | collective-permute-start | bytes 393224 | tf_op jit(solution)/shard_map/ppermute | solution.py:25
  493.0 1.3 copy-start.8
  496.5 1.6 copy-start.7
  501.8 2.0 copy-start.3
  504.4 22.1 %collective-permute-start.2 = (bf16[2,1,128,256]{3,2,1,0:T(8,128)(2,1)}, bf16[2,1,128,256]{3,2,1,0:T(8,128)(2,1)S(1)}, u32[]{:S(2)}, u32[]{:S(2)}) collective-permute-start(bf16[2,1,128,256]{3,2,1,0:T(8,128)(2,1)} %get-tuple-element.140), channel_id=1, source_target_pairs={{0,1},{1,2},{2,3},{3,4},{4,5},{5,6},{6,7},{8,9},{9,10},{10,11},{11... | collective-permute-start | bytes 393224 | tf_op jit(solution)/shard_map/ppermute | solution.py:22
  507.6 19.0 %collective-permute-start.3 = (bf16[2,1,128,256]{3,2,1,0:T(8,128)(2,1)}, bf16[2,1,128,256]{3,2,1,0:T(8,128)(2,1)S(1)}, u32[]{:S(2)}, u32[]{:S(2)}) collective-permute-start(bf16[2,1,128,256]{3,2,1,0:T(8,128)(2,1)} %get-tuple-element.141), channel_id=1, source_target_pairs={{1,0},{2,1},{3,2},{4,3},{5,4},{6,5},{7,6},{9,8},{10,9},{11,10},{12... | collective-permute-start | bytes 393224 | tf_op jit(solution)/shard_map/ppermute | solution.py:25
  535.3 2.2 copy-start.4
  540.3 2.2 copy-start.6
  542.5 2.2 copy-start.1
Sparse Core Ops, SparseCore 0:
  8.9 84.4 all-gather.2
  121.7 85.3 all-gather.4
where the time goes:
time: 563 us; the launch traced here: 552 us
  local copies, waits for them, and re-layouts  193 us (34%)
  waiting for transfers between devices  189 us (34%)
  matrix products  114 us (20%)
  other arithmetic  26.7 us (5%)
  starting transfers between devices  14.9 us (3%)
  between operations  14.3 us (3%)
    all_gather x1, waiting for transfers between devices, on_device(): piece = lax.all_gather(tokens, 'head', axis=1, tiled=True)  86.2 us
    all_gather x1, waiting for transfers between devices, on_device(): all_pairs = lax.all_gather(own_pairs, 'frame', axis=0, tiled=True)  78.9 us
    gather x4, local copies, waits for them, and re-layouts, attend_padded(): picked = key_values[block_ids]  56.6 us
    reshape x4, local copies, waits for them, and re-layouts, attend_padded(): picked.reshape((groups, slot_total * block_size) + picked.shape[3:])  44.4 us
    dot_general x4, matrix products, attend_padded(): jnp.einsum('gihe,gjhe->ghij', queries, picked, precision=highest) * factor  36.1 us
    dot_general x4, matrix products, attend_padded(): blended = jnp.einsum('ghij,gjhe->gihe', weights, picked, precision=highest)  32.1 us
    all_to_all x1, waiting for transfers between devices, on_device(): lax.all_to_all(attended, 'head', split_axis=1, concat_axis=3, tiled=True)  22.9 us
    dot_general x1, matrix products, on_device(): jnp.dot(rows_flat, columns, precision=highest, preferred_element_type=jnp...  22.6 us
  transfers between devices with their start and end apart: 7, of which 3 were waited for; matrix products, arithmetic and copies ran while one was open for 6% of the time, Pallas kernels for 0%

commit v1 on v0

v1 whole, which is shorter than its diff:
```python
import functools

import jax
import jax.numpy as jnp
from jax import lax
from jax.experimental import pallas as pl
from jax.experimental.pallas import tpu as pltpu
from jax.sharding import PartitionSpec as P

HEADS = 16
GRID = 32
BLOCK = 128
eps_norm = 1e-05
highest = lax.Precision.HIGHEST
f32 = jnp.float32
bf16 = jnp.bfloat16


def divisor_upto(count, most):
    return max(d for d in range(1, most + 1) if count % d == 0)


def split_hi_lo(value):
    hi = value.astype(bf16)
    return hi, (value - hi.astype(f32)).astype(bf16)


def mxu(a, b):
    return jnp.dot(a, b, preferred_element_type=f32)


def qkv_kernel(local_heads, head_dim, x_ref, w_ref, q_ref, kv_ref, w_hi, w_lo):
    @pl.when(pl.program_id(0) == 0)
    def _():
        hi, lo = split_hi_lo(w_ref[...])
        w_hi[...] = hi
        w_lo[...] = lo

    x_hi, x_lo = split_hi_lo(x_ref[...])
    acc = mxu(x_hi, w_lo[...]) + mxu(x_lo, w_hi[...])
    acc = acc + mxu(x_hi, w_hi[...])
    pair = 2 * head_dim
    rows = acc.shape[0]
    first = lax.broadcasted_iota(jnp.int32, (rows, pair), 1) < head_dim
    factor = head_dim ** (-0.5)
    for h in range(local_heads):
        both = acc[:, h * pair : (h + 1) * pair]
        turned = pltpu.roll(both, head_dim, 1)
        query = jnp.where(first, both, turned) * factor
        key = jnp.where(first, turned, both)
        q_hi, q_lo = split_hi_lo(query)
        k_hi, k_lo = split_hi_lo(key)
        q_ref[:, 2 * h * pair : (2 * h + 1) * pair] = q_hi
        q_ref[:, (2 * h + 1) * pair : (2 * h + 2) * pair] = q_lo
        kv_ref[:, h * pair : (h + 1) * pair] = jnp.where(first, k_hi.astype(f32), k_lo.astype(f32)).astype(bf16)
    kv_ref[:, local_heads * pair :] = acc[:, local_heads * pair :].astype(bf16)


def project(rows, weight, local_heads, head_dim):
    total, width = rows.shape
    tile = 256
    columns = weight.shape[1]
    return pl.pallas_call(
        functools.partial(qkv_kernel, local_heads, head_dim),
        grid=(total // tile,),
        in_specs=[
            pl.BlockSpec((tile, width), lambda i: (i, 0)),
            pl.BlockSpec((width, columns), lambda i: (0, 0)),
        ],
        out_specs=[
            pl.BlockSpec((tile, local_heads * 4 * head_dim), lambda i: (i, 0)),
            pl.BlockSpec((tile, columns), lambda i: (i, 0)),
        ],
        out_shape=[
            jax.ShapeDtypeStruct((total, local_heads * 4 * head_dim), bf16),
            jax.ShapeDtypeStruct((total, columns), bf16),
        ],
        scratch_shapes=[pltpu.VMEM((width, columns), bf16)] * 2,
        compiler_params=pltpu.CompilerParams(vmem_limit_bytes=48 << 20),
        name="qkv",
    )(rows, weight)


def attend_kernel(local_heads, head_dim, span, lists, counts, q_ref, kv_ref, o_ref):
    b = pl.program_id(0)
    count = counts[b]
    pair = 2 * head_dim
    v_at = local_heads * pair
    v_width = local_heads * head_dim
    stacked = [
        jnp.concatenate(
            [
                q_ref[:, 2 * h * pair : (2 * h + 1) * pair],
                q_ref[:, (2 * h + 1) * pair : (2 * h + 2) * pair],
            ],
            axis=0,
        )
        for h in range(local_heads)
    ]

    def chunk(c, carry):
        offsets = []
        valid = []
        for t in range(span):
            slot = c * span + t
            block = lists[b, jnp.minimum(slot, count - 1)]
            offsets.append(pl.multiple_of(block * BLOCK, BLOCK))
            valid.append(slot < count)
        values = jnp.concatenate(
            [kv_ref[pl.ds(at, BLOCK), v_at : v_at + v_width] for at in offsets], axis=0
        )
        out = []
        for h in range(local_heads):
            top, total, blend = carry[h]
            scores = []
            for at, ok in zip(offsets, valid):
                keys = kv_ref[pl.ds(at, BLOCK), h * pair : (h + 1) * pair]
                both = lax.dot_general(
                    stacked[h], keys, (((1,), (1,)), ((), ())), preferred_element_type=f32
                )
                scores.append(jnp.where(ok, both[:BLOCK] + both[BLOCK:], -jnp.inf))
            peak = functools.reduce(jnp.maximum, scores)
            new_top = jnp.maximum(top, jnp.max(peak, axis=1, keepdims=True))
            scale = jnp.exp(top - new_top)
            weights = [jnp.exp(s - new_top) for s in scores]
            total = total * scale + functools.reduce(jnp.add, weights)
            packed = jnp.concatenate([w.astype(bf16) for w in weights], axis=1)
            blend = blend * scale + mxu(packed, values)
            out.append((new_top, total, blend))
        return tuple(out)

    start = tuple(
        (
            jnp.full((BLOCK, 1), -jnp.inf, f32),
            jnp.zeros((BLOCK, BLOCK), f32),
            jnp.zeros((BLOCK, v_width), f32),
        )
        for _ in range(local_heads)
    )
    final = lax.fori_loop(0, (count + span - 1) // span, chunk, start)
    owner = lax.broadcasted_iota(jnp.int32, (BLOCK, v_width), 1) // head_dim
    result = jnp.zeros((BLOCK, v_width), f32)
    for h in range(local_heads):
        _, total, blend = final[h]
        ready = blend / jnp.sum(total, axis=1, keepdims=True)
        result = jnp.where(owner == h, ready, result)
    o_ref[...] = result.astype(bf16)


def attend(queries, pairs, lists, counts, local_heads, head_dim):
    blocks, slots = lists.shape
    span = -(-slots // (-(-slots // 7)))
    width = local_heads * head_dim
    return pl.pallas_call(
        functools.partial(attend_kernel, local_heads, head_dim, span),
        grid_spec=pltpu.PrefetchScalarGridSpec(
            num_scalar_prefetch=2,
            grid=(blocks,),
            in_specs=[
                pl.BlockSpec((BLOCK, queries.shape[1]), lambda i, *_: (i, 0)),
                pl.BlockSpec(pairs.shape, lambda i, *_: (0, 0), pipeline_mode=pl.Buffered(1)),
            ],
            out_specs=pl.BlockSpec((BLOCK, width), lambda i, *_: (i, 0)),
        ),
        out_shape=jax.ShapeDtypeStruct((blocks * BLOCK, width), bf16),
        compiler_params=pltpu.CompilerParams(vmem_limit_bytes=48 << 20),
        name="attend",
    )(lists, counts, queries, pairs)


def head_kernel(
    token_rows, place, feat_ref, up_ref, conv_ref, bias_ref, out_ref, up_map, act_map, hid_map, flat
):
    channels = feat_ref.shape[-1]
    ext = token_rows + 2
    pixel_cols = 4 * GRID
    feat = feat_ref[0]
    for a in range(4):
        for e in range(4):
            at = (4 * a + e) * channels
            lifted = mxu(feat, up_ref[:, at : at + channels]).astype(bf16)
            for r in range(ext):
                piece = lifted[r * GRID : (r + 1) * GRID]
                up_map[4 * r + a, e * GRID : (e + 1) * GRID, :] = piece
                act_map[4 * r + a, e * GRID : (e + 1) * GRID, :] = jnp.maximum(
                    piece, jnp.zeros((), bf16)
                )

    def conv_rows(source, first, rows, which):
        taps = jnp.concatenate(
            [
                source[pl.ds(first + dy, rows)].reshape(rows * pixel_cols, channels)
                for dy in range(3)
            ],
            axis=1,
        )
        part = []
        for dx in range(3):
            weight = jnp.concatenate([conv_ref[which, dy, dx] for dy in range(3)], axis=0)
            part.append(mxu(taps, weight).reshape(rows, 4, GRID, channels))
        column = lax.broadcasted_iota(jnp.int32, (rows * GRID, channels), 0) % GRID

        def moved(block, step):
            block = block.reshape(rows * GRID, channels)
            turned = pltpu.roll(block, step % (rows * GRID), 0)
            rim = 0 if step > 0 else GRID - 1
            return jnp.where(column == rim, 0.0, turned).reshape(rows, GRID, channels)

        left, centre, right = part
        shifted = []
        for e in range(4):
            low = left[:, e - 1] if e > 0 else moved(left[:, 3], 1)
            high = right[:, e + 1] if e < 3 else moved(right[:, 0], -1)
            shifted.append(low + centre[:, e] + high + bias_ref[which][None, None, :])
        return shifted

    hidden_rows = 4 * token_rows + 2
    group = divisor_upto(hidden_rows, 6)
    top = place[0] == 0
    bottom = place[0] == place[1] - 1
    for g in range(hidden_rows // group):
        pieces = conv_rows(act_map, g * group + 2, group, 0)
        for e in range(4):
            value = jnp.maximum(pieces[e], 0.0).astype(bf16)
            hid_map[g * group : (g + 1) * group, e * GRID : (e + 1) * GRID, :] = value

    @pl.when(top)
    def _():
        hid_map[0] = jnp.zeros((pixel_cols, channels), bf16)

    @pl.when(bottom)
    def _():
        hid_map[hidden_rows - 1] = jnp.zeros((pixel_cols, channels), bf16)

    out_rows = 4 * token_rows
    group2 = divisor_upto(out_rows, 4)
    lanes = 128
    for g in range(out_rows // group2):
        pieces = conv_rows(hid_map, g * group2, group2, 1)
        for r in range(group2):
            y = g * group2 + r
            for e in range(4):
                value = pieces[e][r] + up_map[y + 4, e * GRID : (e + 1) * GRID, :].astype(f32)
                for n in range(channels // lanes):
                    flat[y % 2, n, pl.ds(e, GRID, stride=4), :] = value[:, n * lanes : (n + 1) * lanes]
            for n in range(channels // lanes):
                out_ref[0, y, :, n * lanes : (n + 1) * lanes] = flat[y % 2, n].astype(bf16)


def predict(features, up_weight, conv_weight, conv_bias, place, token_rows):
    frames, ext_tokens, channels = features.shape
    pixel_rows, pixel_cols = 4 * token_rows, 4 * GRID
    once = pl.Buffered(1)
    return pl.pallas_call(
        functools.partial(head_kernel, token_rows),
        grid_spec=pltpu.PrefetchScalarGridSpec(
            num_scalar_prefetch=1,
            grid=(frames,),
            in_specs=[
                pl.BlockSpec((1, ext_tokens, channels), lambda i, *_: (i, 0, 0)),
                pl.BlockSpec(up_weight.shape, lambda i, *_: (0, 0), pipeline_mode=once),
                pl.BlockSpec(conv_weight.shape, lambda i, *_: (0, 0, 0, 0, 0), pipeline_mode=once),
                pl.BlockSpec(conv_bias.shape, lambda i, *_: (0, 0), pipeline_mode=once),
            ],
            out_specs=pl.BlockSpec(
                (1, pixel_rows, pixel_cols, channels), lambda i, *_: (i, 0, 0, 0)
            ),
            scratch_shapes=[
                pltpu.VMEM((pixel_rows + 8, pixel_cols, channels), bf16),
                pltpu.VMEM((pixel_rows + 8, pixel_cols, channels), bf16),
                pltpu.VMEM((pixel_rows + 2, pixel_cols, channels), bf16),
                pltpu.VMEM((2, channels // 128, pixel_cols, 128), f32),
            ],
        ),
        out_shape=jax.ShapeDtypeStruct((frames, pixel_rows, pixel_cols, channels), bf16),
        compiler_params=pltpu.CompilerParams(vmem_limit_bytes=56 << 20),
        name="head",
    )(place, features, up_weight, conv_weight, conv_bias)


def layer_norm(rows, gain):
    centre = jnp.mean(rows, axis=-1, keepdims=True)
    centred = rows - centre
    spread = jnp.mean(centred * centred, axis=-1, keepdims=True)
    return centred * lax.rsqrt(spread + eps_norm) * gain


def local_columns(qkv_weight, local_heads, head_dim):
    width = local_heads * 3 * head_dim
    columns = lax.dynamic_slice_in_dim(qkv_weight, lax.axis_index("head") * width, width, 1)
    columns = columns.reshape(-1, local_heads, 3 * head_dim)
    pairs = columns[:, :, : 2 * head_dim].reshape(-1, local_heads * 2 * head_dim)
    values = columns[:, :, 2 * head_dim :].reshape(-1, local_heads * head_dim)
    return jnp.concatenate([pairs, values], axis=1)


def on_device(
    tokens,
    qkv_weight,
    out_weight,
    norm_gain,
    proj_weight,
    up_weight,
    conv_weight,
    conv_bias,
    block_lists,
    block_counts,
):
    local_frames, strip_tokens, model_width = tokens.shape
    head_groups = lax.axis_size("head")
    local_heads = HEADS // head_groups
    head_dim = model_width // HEADS
    frame_tokens = strip_tokens * head_groups
    weight = local_columns(qkv_weight, local_heads, head_dim)
    rows = lax.all_gather(tokens, "head", axis=1, tiled=True).reshape(-1, model_width)
    queries, own_pairs = project(rows, weight, local_heads, head_dim)
    all_pairs = lax.all_gather(own_pairs, "frame", axis=0, tiled=True)
    attended = attend(queries, all_pairs, block_lists, block_counts, local_heads, head_dim)
    attended = attended.reshape(local_frames, head_groups, strip_tokens, local_heads * head_dim)
    attended = lax.all_to_all(attended, "head", split_axis=1, concat_axis=3, tiled=True)
    attended = attended.reshape(-1, model_width)
    stream = tokens.reshape(-1, model_width) + jnp.dot(
        attended.astype(f32), out_weight, precision=highest, preferred_element_type=f32
    )
    normed = layer_norm(stream, norm_gain)
    features = jnp.dot(
        normed, proj_weight, precision=highest, preferred_element_type=f32
    ).astype(bf16)
    channels = features.shape[1]
    features = features.reshape(local_frames, strip_tokens, channels)
    forward = [(i, i + 1) for i in range(head_groups - 1)]
    backward = [(i + 1, i) for i in range(head_groups - 1)]
    above = lax.ppermute(features[:, strip_tokens - GRID :], "head", forward)
    below = lax.ppermute(features[:, :GRID], "head", backward)
    extended = jnp.concatenate([above, features, below], axis=1)
    place = jnp.stack(
        [lax.axis_index("head").astype(jnp.int32), jnp.full((), head_groups, jnp.int32)]
    )
    return predict(extended, up_weight, conv_weight, conv_bias, place, strip_tokens // GRID)


def solution(mesh):
    in_specs = (
        P("frame", "head", None),
        P(),
        P(),
        P(),
        P(),
        P(),
        P(),
        P(),
        P("frame", None),
        P("frame"),
    )
    out_specs = P("frame", "head", None, None)
    return jax.shard_map(
        on_device, mesh=mesh, in_specs=in_specs, out_specs=out_specs, check_vma=False
    )
```

time: 563 us -> 268 us (0.48); the launches traced: 552 us -> 268 us
  local copies, waits for them, and re-layouts: 193 us -> 12.9 us
  matrix products: 114 us -> 3.53 us
  Pallas kernels: 0 us -> 63.2 us
  waiting for transfers between devices: 189 us -> 148 us
  other arithmetic: 26.7 us -> 2.91 us
  blocking collectives: 0 us -> 19.7 us
  starting transfers between devices: 14.9 us -> 4.55 us
    dot_general x30 -> x2, matrix products: 114 us -> 3.53 us  [the longest x1 2.37 us: on_device(): jnp.dot(attended.astype(f32), out_weight, precision=highest, preferred_el...]
    pallas_call x0 -> x3, Pallas kernels: none -> 63.2 us  [the longest x1 31.3 us: attend(): pl.pallas_call(functools.partial(attend_kernel, local_heads, head_dim, sp...]
    gather x4 -> x0, local copies, waits for them, and re-layouts: 56.6 us -> none  [attend_padded(): picked = key_values[block_ids]]
    reshape x7 -> x2, local copies, waits for them, and re-layouts: 58.2 us -> 2.81 us  [the longest x1 2.63 us: local_columns(): pairs = columns[:, :, :2 * head_dim].reshape(-1, local_heads * 2 * head_dim)]
    all_to_all x1 -> x0, waiting for transfers between devices: 22.9 us -> none  [on_device(): lax.all_to_all(attended, 'head', split_axis=1, concat_axis=3, tiled=True)]
    slice x14 -> x3, local copies, waits for them, and re-layouts: 23.4 us -> 1.09 us  [the longest x1 1.04 us: local_columns(): pairs = columns[:, :, :2 * head_dim].reshape(-1, local_heads * 2 * head_dim)]
    all_to_all x0 -> x1, blocking collectives: none -> 19.7 us  [on_device(): lax.all_to_all(attended, 'head', split_axis=1, concat_axis=3, tiled=True)]
    convert_element_type x3 -> x0, local copies, waits for them, and re-layouts: 17 us -> none  [on_device(): return (upsampled.astype(jnp.float32) + second).astype(jnp.bfloat16)]
  transfers between devices with their start and end apart: 7 -> 4, of which waited for: 3 -> 3; matrix products, arithmetic and copies ran while one was open for 6% -> 4% of each run, Pallas kernels for 0% -> 0%
where the time goes in v1:
time: 268 us
  waiting for transfers between devices  148 us (55%)
  Pallas kernels  63.2 us (24%)
  blocking collectives  19.7 us (7%)
  between operations  13.6 us (5%)
  local copies, waits for them, and re-layouts  12.9 us (5%)
  starting transfers between devices  4.55 us (2%)
  matrix products  3.53 us (1%)
  other arithmetic  2.91 us (1%)
    all_gather x1, waiting for transfers between devices, on_device(): lax.all_gather(tokens, 'head', axis=1, tiled=True).reshape(-1, model_width)  76.4 us
    all_gather x1, waiting for transfers between devices, on_device(): all_pairs = lax.all_gather(own_pairs, 'frame', axis=0, tiled=True)  68.1 us
    pallas_call x1, Pallas kernels, attend(): pl.pallas_call(functools.partial(attend_kernel, local_heads, head_dim, sp...  31.3 us
    pallas_call x1, Pallas kernels, predict(): pl.pallas_call(functools.partial(head_kernel, token_rows), grid_spec=pltp...  21.1 us
    all_to_all x1, blocking collectives, on_device(): lax.all_to_all(attended, 'head', split_axis=1, concat_axis=3, tiled=True)  19.7 us
    pallas_call x1, Pallas kernels, project(): pl.pallas_call(functools.partial(qkv_kernel, local_heads, head_dim), grid...  10.8 us
    unnamed x19, local copies, waits for them, and re-layouts  5.96 us
  transfers between devices with their start and end apart: 4, of which 3 were waited for; matrix products, arithmetic and copies ran while one was open for 4% of the time, Pallas kernels for 0%

profile of v1, /device:TPU:1, one launch (start us, length us, event | category | flops | bytes accessed | tf_op | source)
XLA Modules:
  0.0 267.9 jit_solution(4787625873249123191)
XLA Ops:
  6.5 0.7 all-gather.3.cloned.1.call-update
  7.3 0.0 all-gather.5.cloned.1.call-start
  7.3 2.7 constant_dynamic-slice_fusion
  10.0 1.9 copy.21
  11.9 1.0 slice.16
  12.9 2.6 copy.20
  15.6 0.2 copy.17
  15.8 1.3 pad_maximum_fusion.w_ref
  17.1 76.4 %all-gather.3.cloned.1.call-done = f32[2,1024,1024]{2,1,0:T(8,128)} async-done(((f32[2,128,1024]{2,1,0:T(8,128)}), f32[2,1024,1024]{2,1,0:T(8,128)}) %all-gather.3.cloned.1.call-update) | async-done | bytes 8388624 | tf_op jit(solution)/shard_map/all_gather | solution.py:315
  93.5 10.8 %qkv.1 = (bf16[2048,512]{1,0:T(8,128)(2,1)S(1)}, bf16[2048,384]{1,0:T(8,128)(2,1)S(1)}) custom-call(f32[2048,1024]{1,0:T(8,128)} %bitcast.22, f32[1024,384]{1,0:T(8,128)S(1)} %pad_maximum_fusion.w_ref), custom_call_target="tpu_custom_call" | custom-call | tf_op jit(solution)/shard_map/qkv/pallas_call | solution.py:63
  104.3 0.0 copy-start.1
  104.3 1.3 copy-done.1
  105.6 1.1 copy-done.3
  106.8 0.0 all-gather.5.cloned.1.call-update
  106.8 68.1 %all-gather.5.cloned.1.call-done.kv_ref = bf16[8192,384]{1,0:T(8,128)(2,1)} async-done(((bf16[2048,384]{1,0:T(8,128)(2,1)}), bf16[8192,384]{1,0:T(8,128)(2,1)}) %all-gather.5.cloned.1.call-update) | async-done | bytes 6291472 | tf_op jit(solution)/shard_map/all_gather | solution.py:317
  174.9 1.6 copy-done.2
  176.5 31.3 %attend.1 = bf16[2048,128]{1,0:T(8,128)(2,1)S(1)} custom-call(s32[16,13]{1,0:T(8,128)S(1)} %copy-done.4, s32[16]{0:T(128)S(1)} %copy-done.5, bf16[2048,512]{1,0:T(8,128)(2,1)S(1)} %copy-done.2, bf16[8192,384]{1,0:T(8,128)(2,1)} %all-gather.5.cloned.1.call-done.kv_ref), custom_call_target="tpu_custom_call" | custom-call | tf_op jit(solution)/shard_map/attend/pallas_call | solution.py:154
  207.8 0.0 copy-start.7
  207.8 19.7 %all_to_all.15 = bf16[2,8,128,128]{3,2,0,1:T(8,128)(2,1)S(1)} all-to-all(bf16[2,8,128,128]{3,2,0,1:T(8,128)(2,1)S(1)} %copy.18), channel_id=1, replica_groups=mesh['frame'=4,'head'=8] {'head'}, dimensions={1} | all-to-all | bytes 1048576 | tf_op jit(solution)/shard_map/all_to_all | solution.py:320
  227.5 0.3 copy.19
  227.9 0.0 copy-start.8
  227.9 2.4 fusion.9
  230.3 0.3 multiply_reduce_fusion
  230.5 0.0 copy-done
  230.5 1.2 convolution_convert_fusion
  231.7 2.3 collective-permute-start
  234.0 2.2 collective-permute-start.1
  236.2 0.6 pad_add_fusion.place
  236.8 0.0 collective-permute-done
  236.8 2.4 collective-permute-done.1
  239.2 0.7 pad_maximum_fusion.1.feat_ref
  239.9 21.1 %head.1 = bf16[2,16,128,256]{3,2,1,0:T(8,128)(2,1)} custom-call(s32[2]{0:T(128)} %pad_add_fusion.place, bf16[2,192,256]{2,1,0:T(8,128)(2,1)} %pad_maximum_fusion.1.feat_ref, bf16[256,4096]{1,0:T(8,128)(2,1)} %up_ref.1, bf16[2,3,3,256,256]{4,3,2,1,0:T(8,128)(2,1)} %conv_ref.1, f32[2,256]{1,0:T(2,128)} %bias_ref.1), custom_call_target="tpu_custom_call" | custom-call | tf_op jit(solution)/shard_map/head/pallas_call | solution.py:254
  (17 shorter events, 0.1 us)
Async XLA Ops:
  6.5 224.0 %copy-start = (f32[1024,256]{1,0:T(8,128)S(1)}, f32[1024,256]{1,0:T(8,128)}, u32[]{:S(2)}) copy-start(f32[1024,256]{1,0:T(8,128)} %param.14) | copy-start | bytes 3145732
  6.5 86.9 %all-gather.3.cloned.1.call-start = ((), (), s32[]{:S(2)}) async-start(), calls=%async_computation.1 | async-start | bytes 9437184 | tf_op jit(solution)/shard_map/all_gather | solution.py:315
  7.3 167.6 %all-gather.5.cloned.1.call-start = ((), (), s32[]{:S(2)}) async-start(), calls=%async_computation.2 | async-start | bytes 7864320 | tf_op jit(solution)/shard_map/all_gather | solution.py:317
  93.5 81.4 %copy-start.4 = (s32[16,13]{1,0:T(8,128)S(1)}, s32[16,13]{1,0:T(8,128)}, u32[]{:S(2)}) copy-start(s32[16,13]{1,0:T(8,128)} %lists.1) | copy-start | bytes 2500
  93.5 81.4 %copy-start.5 = (s32[16]{0:T(128)S(1)}, s32[16]{0:T(128)}, u32[]{:S(2)}) copy-start(s32[16]{0:T(128)} %counts.1) | copy-start | bytes 196
  104.3 1.3 copy-start.1
  105.6 1.2 copy-start.3
  174.9 1.6 copy-start.2
  176.5 51.4 %copy-start.6 = (f32[1024,1024]{1,0:T(8,128)S(1)}, f32[1024,1024]{1,0:T(8,128)}, u32[]{:S(2)}) copy-start(f32[1024,1024]{1,0:T(8,128)} %param.12) | copy-start | bytes 12582916
  207.8 20.1 %copy-start.7 = (f32[2,128,1024]{2,1,0:T(8,128)S(1)}, f32[2,128,1024]{2,1,0:T(8,128)}, u32[]{:S(2)}) copy-start(f32[2,128,1024]{2,1,0:T(8,128)} %param.10) | copy-start | bytes 3145732
  227.9 2.7 copy-start.8
  231.7 5.1 %collective-permute-start = (bf16[2,32,256]{2,1,0:T(8,128)(2,1)S(1)}, bf16[2,32,256]{2,1,0:T(8,128)(2,1)S(1)}, u32[]{:S(2)}, u32[]{:S(2)}) collective-permute-start(bf16[2,32,256]{2,1,0:T(8,128)(2,1)S(1)} %get-tuple-element.9), channel_id=1, source_target_pairs={{0,1},{1,2},{2,3},{3,4},{4,5},{5,6},{6,7},{8,9},{9,10},{10,11},{11... | collective-permute-start | bytes 98312 | tf_op jit(solution)/shard_map/ppermute | solution.py:333
  234.0 5.2 %collective-permute-start.1 = (bf16[2,32,256]{2,1,0:T(8,128)(2,1)S(1)}, bf16[2,32,256]{2,1,0:T(8,128)(2,1)S(1)}, u32[]{:S(2)}, u32[]{:S(2)}) collective-permute-start(bf16[2,32,256]{2,1,0:T(8,128)(2,1)S(1)} %get-tuple-element.10), channel_id=1, source_target_pairs={{1,0},{2,1},{3,2},{4,3},{5,4},{6,5},{7,6},{9,8},{10,9},{11,10},{12... | collective-permute-start | bytes 98312 | tf_op jit(solution)/shard_map/ppermute | solution.py:334
Sparse Core Ops, SparseCore 0:
  8.9 84.4 all-gather.2
  106.9 67.9 all-gather.4

commit v2 on v1

--- a/solution.py
+++ b/solution.py
@@ -29,56 +29,240 @@
     return jnp.dot(a, b, preferred_element_type=f32)
 
 
-def qkv_kernel(local_heads, head_dim, x_ref, w_ref, q_ref, kv_ref, w_hi, w_lo):
+def qkv_kernel(local_heads, head_dim, x_ref, w_ref, q_ref, kv_ref, x_hi, x_lo):
     @pl.when(pl.program_id(0) == 0)
     def _():
-        hi, lo = split_hi_lo(w_ref[...])
-        w_hi[...] = hi
-        w_lo[...] = lo
-
-    x_hi, x_lo = split_hi_lo(x_ref[...])
-    acc = mxu(x_hi, w_lo[...]) + mxu(x_lo, w_hi[...])
-    acc = acc + mxu(x_hi, w_hi[...])
+        hi, lo = split_hi_lo(x_ref[...])
+        x_hi[...] = hi
+        x_lo[...] = lo
+
+    w_hi, w_lo = split_hi_lo(w_ref[...])
+    acc = mxu(x_hi[...], w_lo) + mxu(x_lo[...], w_hi)
+    acc = acc + mxu(x_hi[...], w_hi)
     pair = 2 * head_dim
-    rows = acc.shape[0]
+    frames, _, strip, _ = q_ref.shape
+    rows = frames * strip
     first = lax.broadcasted_iota(jnp.int32, (rows, pair), 1) < head_dim
+    parts = [acc[:, n * pair : (n + 1) * pair] for n in range(3)]
+    turned = [pltpu.roll(part, head_dim, 1) for part in parts]
+
+    def coded(value):
+        rest = value - value.astype(bf16).astype(f32)
+        return jnp.where(first, value, rest).astype(bf16).reshape(frames, strip, pair)
+
     factor = head_dim ** (-0.5)
-    for h in range(local_heads):
-        both = acc[:, h * pair : (h + 1) * pair]
-        turned = pltpu.roll(both, head_dim, 1)
-        query = jnp.where(first, both, turned) * factor
-        key = jnp.where(first, turned, both)
-        q_hi, q_lo = split_hi_lo(query)
-        k_hi, k_lo = split_hi_lo(key)
-        q_ref[:, 2 * h * pair : (2 * h + 1) * pair] = q_hi
-        q_ref[:, (2 * h + 1) * pair : (2 * h + 2) * pair] = q_lo
-        kv_ref[:, h * pair : (h + 1) * pair] = jnp.where(first, k_hi.astype(f32), k_lo.astype(f32)).astype(bf16)
-    kv_ref[:, local_heads * pair :] = acc[:, local_heads * pair :].astype(bf16)
-
-
-def project(rows, weight, local_heads, head_dim):
-    total, width = rows.shape
-    tile = 256
-    columns = weight.shape[1]
+    queries = [
+        coded(jnp.where(first, parts[0], turned[0]) * factor),
+        coded(jnp.where(first, turned[1], parts[1]) * factor),
+    ]
+    keys = [
+        coded(jnp.where(first, turned[0], parts[0])),
+        coded(jnp.where(first, parts[2], turned[2])),
+    ]
+    if local_heads == 2:
+        for h in range(2):
+            q_ref[:, 0, :, h * pair : (h + 1) * pair] = queries[h]
+            kv_ref[:, 0, :, h * pair : (h + 1) * pair] = keys[h]
+        values = jnp.where(first, parts[1], parts[2]).astype(bf16)
+        kv_ref[:, 0, :, 2 * pair :] = values.reshape(frames, strip, pair)
+    else:
+        for h, values in enumerate((parts[1], turned[2])):
+            q_ref[:, h] = queries[h]
+            kv_ref[:, h, :, :pair] = keys[h]
+            values = values[:, :head_dim].astype(bf16)
+            kv_ref[:, h, :, pair:] = values.reshape(frames, strip, head_dim)
+
+
+def project(tokens, weight, head_groups, head_dim):
+    frames, strip, width = tokens.shape
+    local_heads = HEADS // head_groups
+    share = 2 // local_heads
+    columns = 6 * head_dim
+    q_width, kv_width = local_heads * 2 * head_dim, local_heads * 3 * head_dim
     return pl.pallas_call(
         functools.partial(qkv_kernel, local_heads, head_dim),
-        grid=(total // tile,),
+        grid=(HEADS // 2,),
         in_specs=[
-            pl.BlockSpec((tile, width), lambda i: (i, 0)),
-            pl.BlockSpec((width, columns), lambda i: (0, 0)),
+            pl.BlockSpec((frames * strip, width), lambda i: (0, 0)),
+            pl.BlockSpec((width, columns), lambda i: (0, i)),
         ],
         out_specs=[
-            pl.BlockSpec((tile, local_heads * 4 * head_dim), lambda i: (i, 0)),
-            pl.BlockSpec((tile, columns), lambda i: (i, 0)),
+            pl.BlockSpec((frames, share, strip, q_width), lambda i: (0, i, 0, 0)),
+            pl.BlockSpec((frames, share, strip, kv_width), lambda i: (0, i, 0, 0)),
         ],
         out_shape=[
-            jax.ShapeDtypeStruct((total, local_heads * 4 * head_dim), bf16),
-            jax.ShapeDtypeStruct((total, columns), bf16),
+            jax.ShapeDtypeStruct((frames, head_groups, strip, q_width), bf16),
+            jax.ShapeDtypeStruct((frames, head_groups, strip, kv_width), bf16),
         ],
-        scratch_shapes=[pltpu.VMEM((width, columns), bf16)] * 2,
+        scratch_shapes=[pltpu.VMEM((frames * strip, width), bf16)] * 2,
         compiler_params=pltpu.CompilerParams(vmem_limit_bytes=48 << 20),
         name="qkv",
-    )(rows, weight)
+    )(tokens.reshape(-1, width), weight)
+
+
+MESH = pl.DeviceIdType.MESH
+
+
+def near_first(count):
+    return sorted(range(1, count), key=lambda j: (min(j, count - j), j))
+
+
+def greet(peers):
+    barrier = pltpu.get_barrier_semaphore()
+    for peer in peers:
+        pl.semaphore_signal(barrier, inc=1, device_id=peer, device_id_type=MESH)
+    pl.semaphore_wait(barrier, len(peers))
+
+
+def exchange_kernel(
+    groups, teams, q_ref, kv_ref, q_out, pairs, own_sem,
+    q_send, q_recv, z_send, z_recv, f_send, f_recv, r_send, r_recv,
+):
+    frames = q_ref.shape[0]
+    team, me = lax.axis_index("frame"), lax.axis_index("head")
+    square = teams == 4
+    if square:
+        side = lax.rem(team, 2)
+        beside, across = team + 1 - 2 * side, lax.rem(team + 2, 4)
+        direct = [(beside, beside), (across, across)]
+    else:
+        direct = [
+            (lax.rem(team + k, teams), lax.rem(team + teams - k, teams)) for k in range(1, teams)
+        ]
+    order = near_first(groups)
+    peers = [(team, lax.rem(me + j, groups)) for j in order] + [(to, me) for to, _ in direct]
+    greet(peers)
+
+    def remote(src, dst, send, recv, target):
+        return pltpu.make_async_remote_copy(
+            src_ref=src, dst_ref=dst, send_sem=send, recv_sem=recv,
+            device_id=target, device_id_type=MESH,
+        )
+
+    def z_copy(f, j):
+        to = lax.rem(me + j, groups)
+        return remote(
+            kv_ref.at[f, to], pairs.at[team * frames + f, me],
+            z_send.at[f, j], z_recv.at[f, j], (team, to),
+        )
+
+    def q_copy(f, j):
+        to = lax.rem(me + j, groups)
+        return remote(
+            q_ref.at[f, to], q_out.at[f, me], q_send.at[f, j], q_recv.at[f, j], (team, to)
+        )
+
+    def piece(owner, f, j):
+        return pairs.at[owner * frames + f, lax.rem(me + groups - j, groups)]
+
+    def f_copy(k, f, j):
+        src = kv_ref.at[f, me] if j == 0 else piece(team, f, j)
+        return remote(
+            src, piece(team, f, j), f_send.at[k, f, j], f_recv.at[k, f, j], (direct[k][0], me)
+        )
+
+    def r_copy(f, j):
+        origin, to = (beside, across) if f % 2 == 0 else (across, beside)
+        here = piece(origin, f, j)
+        return remote(here, here, r_send.at[f, j], r_recv.at[f, j], (to, me))
+
+    own = []
+    for f in range(frames):
+        own.append(
+            pltpu.make_async_copy(kv_ref.at[f, me], pairs.at[team * frames + f, me], own_sem.at[0, f])
+        )
+        own.append(pltpu.make_async_copy(q_ref.at[f, me], q_out.at[f, me], own_sem.at[1, f]))
+    schedule = [(f, j) for j in [0] + order for f in range(frames)]
+    for f, j in schedule:
+        if j:
+            z_copy(f, j).start()
+    for f, j in schedule:
+        if j:
+            q_copy(f, j).start()
+    for copy in own:
+        copy.start()
+    lag = 2 * frames
+    for n in range(len(schedule) + lag):
+        if n < len(schedule):
+            f, j = schedule[n]
+            if j:
+                z_copy(f, j).wait_recv()
+            for k in range(len(direct)):
+                f_copy(k, f, j).start()
+        if n >= lag and square:
+            f, j = schedule[n - lag]
+            f_copy(f % 2, f, j).wait_recv()
+            r_copy(f, j).start()
+    for f, j in schedule:
+        for k in range(len(direct)):
+            f_copy(k, f, j).wait_send()
+            if not (square and k == f % 2):
+                f_copy(k, f, j).wait_recv()
+        if square:
+            r_copy(f, j).wait()
+        if j:
+            z_copy(f, j).wait_send()
+            q_copy(f, j).wait()
+    for copy in own:
+        copy.wait()
+
+
+def exchange(queries, own_pairs, groups, teams):
+    frames = queries.shape[0]
+    sems = lambda *shape: pltpu.SemaphoreType.DMA(shape)
+    hops = 2 if teams == 4 else teams - 1
+    vmem = pl.BlockSpec(memory_space=pltpu.VMEM)
+    anywhere = pl.BlockSpec(memory_space=pl.ANY)
+    return pl.pallas_call(
+        functools.partial(exchange_kernel, groups, teams),
+        in_specs=[vmem, vmem],
+        out_specs=[anywhere, anywhere],
+        out_shape=[
+            jax.ShapeDtypeStruct(queries.shape, bf16),
+            jax.ShapeDtypeStruct((teams * frames,) + own_pairs.shape[1:], bf16),
+        ],
+        scratch_shapes=[sems(2, frames)]
+        + [sems(frames, groups)] * 4
+        + [sems(hops, frames, groups)] * 2
+        + [sems(frames, groups)] * 2,
+        compiler_params=pltpu.CompilerParams(collective_id=0, has_side_effects=True),
+        name="exchange",
+    )(queries, own_pairs)
+
+
+def hand_back_kernel(groups, src, dst, own_sem, send, recv):
+    team, me = lax.axis_index("frame"), lax.axis_index("head")
+    order = near_first(groups)
+    greet([(team, lax.rem(me + j, groups)) for j in order])
+    copies = []
+    for j in reversed(order):
+        to = lax.rem(me + j, groups)
+        copies.append(
+            pltpu.make_async_remote_copy(
+                src_ref=src.at[:, to], dst_ref=dst.at[me],
+                send_sem=send.at[j], recv_sem=recv.at[j],
+                device_id=(team, to), device_id_type=MESH,
+            )
+        )
+    copies.append(pltpu.make_async_copy(src.at[:, me], dst.at[me], own_sem))
+    for copy in copies:
+        copy.start()
+    for copy in copies:
+        copy.wait()
+
+
+def hand_back(attended):
+    frames, groups, strip, width = attended.shape
+    vmem = pl.BlockSpec(memory_space=pltpu.VMEM)
+    return pl.pallas_call(
+        functools.partial(hand_back_kernel, groups),
+        in_specs=[vmem],
+        out_specs=vmem,
+        out_shape=jax.ShapeDtypeStruct((groups, frames, strip, width), bf16),
+        scratch_shapes=[pltpu.SemaphoreType.DMA] + [pltpu.SemaphoreType.DMA((groups,))] * 2,
+        compiler_params=pltpu.CompilerParams(collective_id=1, has_side_effects=True),
+        name="hand_back",
+    )(attended)
 
 
 def attend_kernel(local_heads, head_dim, span, lists, counts, q_ref, kv_ref, o_ref):
@@ -87,16 +271,13 @@
     pair = 2 * head_dim
     v_at = local_heads * pair
     v_width = local_heads * head_dim
-    stacked = [
-        jnp.concatenate(
-            [
-                q_ref[:, 2 * h * pair : (2 * h + 1) * pair],
-                q_ref[:, (2 * h + 1) * pair : (2 * h + 2) * pair],
-            ],
-            axis=0,
-        )
-        for h in range(local_heads)
-    ]
+    first = lax.broadcasted_iota(jnp.int32, (BLOCK, pair), 1) < head_dim
+    stacked = []
+    for h in range(local_heads):
+        coded = q_ref[:, h * pair : (h + 1) * pair].astype(f32)
+        turned = pltpu.roll(coded, head_dim, 1)
+        high, low = jnp.where(first, coded, turned), jnp.where(first, turned, coded)
+        stacked.append(jnp.concatenate([high, low], axis=0).astype(bf16))
 
     def chunk(c, carry):
         offsets = []
@@ -285,15 +466,6 @@
     return centred * lax.rsqrt(spread + eps_norm) * gain
 
 
-def local_columns(qkv_weight, local_heads, head_dim):
-    width = local_heads * 3 * head_dim
-    columns = lax.dynamic_slice_in_dim(qkv_weight, lax.axis_index("head") * width, width, 1)
-    columns = columns.reshape(-1, local_heads, 3 * head_dim)
-    pairs = columns[:, :, : 2 * head_dim].reshape(-1, local_heads * 2 * head_dim)
-    values = columns[:, :, 2 * head_dim :].reshape(-1, local_heads * head_dim)
-    return jnp.concatenate([pairs, values], axis=1)
-
-
 def on_device(
     tokens,
     qkv_weight,
@@ -310,15 +482,14 @@
     head_groups = lax.axis_size("head")
     local_heads = HEADS // head_groups
     head_dim = model_width // HEADS
-    frame_tokens = strip_tokens * head_groups
-    weight = local_columns(qkv_weight, local_heads, head_dim)
-    rows = lax.all_gather(tokens, "head", axis=1, tiled=True).reshape(-1, model_width)
-    queries, own_pairs = project(rows, weight, local_heads, head_dim)
-    all_pairs = lax.all_gather(own_pairs, "frame", axis=0, tiled=True)
+    own_queries, own_pairs = project(tokens, qkv_weight, head_groups, head_dim)
+    queries, all_pairs = exchange(own_queries, own_pairs, head_groups, lax.axis_size("frame"))
+    queries = queries.reshape(-1, queries.shape[-1])
+    all_pairs = all_pairs.reshape(-1, all_pairs.shape[-1])
     attended = attend(queries, all_pairs, block_lists, block_counts, local_heads, head_dim)
     attended = attended.reshape(local_frames, head_groups, strip_tokens, local_heads * head_dim)
-    attended = lax.all_to_all(attended, "head", split_axis=1, concat_axis=3, tiled=True)
-    attended = attended.reshape(-1, model_width)
+    attended = hand_back(attended).reshape(head_groups, -1, local_heads * head_dim)
+    attended = jnp.transpose(attended, (1, 0, 2)).reshape(-1, model_width)
     stream = tokens.reshape(-1, model_width) + jnp.dot(
         attended.astype(f32), out_weight, precision=highest, preferred_element_type=f32
     )

time: 268 us -> 169 us (0.63)
  waiting for transfers between devices: 148 us -> 2.5 us
  Pallas kernels: 63.2 us -> 146 us
  blocking collectives: 19.7 us -> 0 us
  between operations: 13.6 us -> 0.16 us
  local copies, waits for them, and re-layouts: 12.9 us -> 6.73 us
    all_gather x2 -> x0, waiting for transfers between devices: 144 us -> none  [the longest x1 76.4 us: on_device(): lax.all_gather(tokens, 'head', axis=1, tiled=True).reshape(-1, model_width)]
    pallas_call x0 -> x2, Pallas kernels: none -> 81.6 us  [the longest x1 65.2 us: exchange(): pl.pallas_call(functools.partial(exchange_kernel, groups, teams), in_spec...]
    all_to_all x1 -> x0, blocking collectives: 19.7 us -> none  [on_device(): lax.all_to_all(attended, 'head', split_axis=1, concat_axis=3, tiled=True)]
    unnamed x19 -> x20, local copies, waits for them, and re-layouts: 5.96 us -> 5.48 us
  transfers between devices with their start and end apart: 4 -> 2, of which waited for: 3 -> 1; matrix products, arithmetic and copies ran while one was open for 4% -> 0% of each run, Pallas kernels for 0% -> 0%
where the time goes in v2:
time: 169 us
  Pallas kernels  146 us (86%)
  local copies, waits for them, and re-layouts  6.73 us (4%)
  starting transfers between devices  5.97 us (4%)
  matrix products  5.69 us (3%)
  waiting for transfers between devices  2.5 us (1%)
    pallas_call x1, Pallas kernels, exchange(): pl.pallas_call(functools.partial(exchange_kernel, groups, teams), in_spec...  65.2 us
    pallas_call x1, Pallas kernels, attend(): pl.pallas_call(functools.partial(attend_kernel, local_heads, head_dim, sp...  32.1 us
    pallas_call x1, Pallas kernels, predict(): pl.pallas_call(functools.partial(head_kernel, token_rows), grid_spec=pltp...  21.1 us
    pallas_call x1, Pallas kernels, hand_back(): pl.pallas_call(functools.partial(hand_back_kernel, groups), in_specs=[vme...  16.4 us
    pallas_call x1, Pallas kernels, project(): pl.pallas_call(functools.partial(qkv_kernel, local_heads, head_dim), grid...  11.6 us
    unnamed x20, local copies, waits for them, and re-layouts  5.48 us
    dot_general x1, matrix products, on_device(): jnp.dot(attended.astype(f32), out_weight, precision=highest, preferred_el...  4.54 us
    ppermute x1, starting transfers between devices, on_device(): above = lax.ppermute(features[:, strip_tokens - GRID:], 'head', forward)  3.87 us
  transfers between devices with their start and end apart: 2, of which 1 were waited for; matrix products, arithmetic and copies ran while one was open for 0% of the time, Pallas kernels for 0%

profile of v2, /device:TPU:1, one launch (start us, length us, event | category | flops | bytes accessed | tf_op | source)
XLA Modules:
  0.0 169.0 jit_solution(2333938069277212802)
XLA Ops:
  0.0 0.0 copy-start
  0.0 0.0 copy-start.1
  0.0 1.3 copy-done.1
  1.3 0.0 copy-start.8
  1.3 11.6 %qkv.1 = (bf16[2,8,128,256]{3,2,1,0:T(8,128)(2,1)S(1)}, bf16[2,8,128,384]{3,2,1,0:T(8,128)(2,1)S(1)}) custom-call(f32[256,1024]{1,0:T(8,128)S(1)} %bitcast.13, f32[1024,3072]{1,0:T(8,128)} %w_ref.1), custom_call_target="tpu_custom_call" | custom-call | tf_op jit(solution)/shard_map/qkv/pallas_call | solution.py:82
  12.9 0.0 copy-start.4
  12.9 1.1 copy-done.4
  14.1 1.0 copy-done.6
  15.1 65.2 %exchange.1 = (bf16[2,8,128,256]{3,2,1,0:T(8,128)(2,1)}, bf16[8,8,128,384]{3,2,1,0:T(8,128)(2,1)}) custom-call(bf16[2,8,128,256]{3,2,1,0:T(8,128)(2,1)} %copy-done.6, bf16[2,8,128,384]{3,2,1,0:T(8,128)(2,1)} %copy-done.4), custom_call_target="tpu_custom_call" | custom-call | tf_op jit(solution)/shard_map/exchange/pallas_call | solution.py:216
  80.3 0.0 copy-done.7
  80.3 0.0 copy-done.8
  80.3 0.0 copy-start.5
  80.3 1.2 copy-done.5
  81.6 32.1 %attend.1 = bf16[2048,128]{1,0:T(8,128)(2,1)S(1)} custom-call(s32[16,13]{1,0:T(8,128)S(1)} %copy-done.7, s32[16]{0:T(128)S(1)} %copy-done.8, bf16[2048,256]{1,0:T(8,128)(2,1)S(1)} %bitcast.16, bf16[8192,384]{1,0:T(8,128)(2,1)} %bitcast.17), custom_call_target="tpu_custom_call" | custom-call | tf_op jit(solution)/shard_map/attend/pallas_call | solution.py:335
  113.7 0.0 copy-start.3
  113.7 0.8 copy-done.3
  114.5 16.4 %hand_back.1 = bf16[8,2,128,128]{3,2,1,0:T(8,128)(2,1)} custom-call(bf16[2,8,128,128]{3,2,1,0:T(8,128)(2,1)} %bitcast.15), custom_call_target="tpu_custom_call" | custom-call | tf_op jit(solution)/shard_map/hand_back/pallas_call | solution.py:257
  130.8 1.2 copy.11
  132.1 0.0 copy-start.9
  132.1 0.0 copy-done.2
  132.1 4.5 %fusion.7 = (f32[256]{0:T(256)S(1)}, f32[256,1024]{1,0:T(8,128)S(1)}) fusion(f32[256,1024]{1,0:T(8,128)S(1)} %bitcast.14, bf16[256,1024]{0,1:T(8,128)(2,1)S(1)} %bitcast.18, f32[1024,1024]{1,0:T(8,128)} %param.12), kind=kOutput, calls=%fused_computation.14 | convolution fusion | flops 3221749504 | bytes 6816768 | tf_op jit(solution)/shard_map/dot_general | solution.py:493
  136.7 0.3 multiply_reduce_fusion
  136.9 0.0 copy-done
  136.9 0.0 copy-done.9
  136.9 1.2 convolution_convert_fusion
  138.1 3.9 %collective-permute-start = (bf16[2,32,256]{2,1,0:T(8,128)(2,1)S(1)}, bf16[2,32,256]{2,1,0:T(8,128)(2,1)S(1)}, u32[]{:S(2)}, u32[]{:S(2)}) collective-permute-start(bf16[2,32,256]{2,1,0:T(8,128)(2,1)S(1)} %get-tuple-element.13), channel_id=1, source_target_pairs={{0,1},{1,2},{2,3},{3,4},{4,5},{5,6},{6,7},{8,9},{9,10},{10,11},{11... | collective-permute-start | bytes 98312 | tf_op jit(solution)/shard_map/ppermute | solution.py:504
  142.0 2.1 %collective-permute-start.1 = (bf16[2,32,256]{2,1,0:T(8,128)(2,1)S(1)}, bf16[2,32,256]{2,1,0:T(8,128)(2,1)S(1)}, u32[]{:S(2)}, u32[]{:S(2)}) collective-permute-start(bf16[2,32,256]{2,1,0:T(8,128)(2,1)S(1)} %get-tuple-element.14), channel_id=1, source_target_pairs={{1,0},{2,1},{3,2},{4,3},{5,4},{6,5},{7,6},{9,8},{10,9},{11,10},{12... | collective-permute-start | bytes 98312 | tf_op jit(solution)/shard_map/ppermute | solution.py:505
  144.1 0.6 pad_add_fusion.place
  144.7 0.0 collective-permute-done
  144.7 2.5 %collective-permute-done.1 = bf16[2,32,256]{2,1,0:T(8,128)(2,1)S(1)} collective-permute-done((bf16[2,32,256]{2,1,0:T(8,128)(2,1)S(1)}, bf16[2,32,256]{2,1,0:T(8,128)(2,1)S(1)}, u32[]{:S(2)}, u32[]{:S(2)}) %collective-permute-start.1) | collective-permute-done | bytes 32800 | tf_op jit(solution)/shard_map/ppermute | solution.py:505
  147.2 0.7 pad_maximum_fusion.feat_ref
  147.9 21.1 %head.1 = bf16[2,16,128,256]{3,2,1,0:T(8,128)(2,1)} custom-call(s32[2]{0:T(128)} %pad_add_fusion.place, bf16[2,192,256]{2,1,0:T(8,128)(2,1)} %pad_maximum_fusion.feat_ref, bf16[256,4096]{1,0:T(8,128)(2,1)} %up_ref.1, bf16[2,3,3,256,256]{4,3,2,1,0:T(8,128)(2,1)} %conv_ref.1, f32[2,256]{1,0:T(2,128)} %bias_ref.1), custom_call_target="tpu_custom_call" | custom-call | tf_op jit(solution)/shard_map/head/pallas_call | solution.py:435
  (6 shorter events, 0.0 us)
Async XLA Ops:
  0.0 136.9 %copy-start = (f32[1024,256]{1,0:T(8,128)S(1)}, f32[1024,256]{1,0:T(8,128)}, u32[]{:S(2)}) copy-start(f32[1024,256]{1,0:T(8,128)} %param.14) | copy-start | bytes 3145732
  0.0 1.3 copy-start.1
  1.3 79.0 %copy-start.7 = (s32[16,13]{1,0:T(8,128)S(1)}, s32[16,13]{1,0:T(8,128)}, u32[]{:S(2)}) copy-start(s32[16,13]{1,0:T(8,128)} %lists.1) | copy-start | bytes 2500
  1.3 79.0 %copy-start.8 = (s32[16]{0:T(128)S(1)}, s32[16]{0:T(128)}, u32[]{:S(2)}) copy-start(s32[16]{0:T(128)} %counts.1) | copy-start | bytes 196
  12.9 1.1 copy-start.4
  14.1 1.0 copy-start.6
  80.3 1.2 copy-start.5
  81.6 50.5 %copy-start.2 = (f32[2,128,1024]{2,1,0:T(8,128)S(1)}, f32[2,128,1024]{2,1,0:T(8,128)}, u32[]{:S(2)}) copy-start(f32[2,128,1024]{2,1,0:T(8,128)} %param.10) | copy-start | bytes 3145732
  113.7 0.8 copy-start.3
  132.1 4.8 %copy-start.9 = (f32[1024]{0:T(1024)S(1)}, f32[1024]{0:T(1024)}, u32[]{:S(2)}) copy-start(f32[1024]{0:T(1024)} %param.13) | copy-start | bytes 12292
  138.1 6.6 %collective-permute-start = (bf16[2,32,256]{2,1,0:T(8,128)(2,1)S(1)}, bf16[2,32,256]{2,1,0:T(8,128)(2,1)S(1)}, u32[]{:S(2)}, u32[]{:S(2)}) collective-permute-start(bf16[2,32,256]{2,1,0:T(8,128)(2,1)S(1)} %get-tuple-element.13), channel_id=1, source_target_pairs={{0,1},{1,2},{2,3},{3,4},{4,5},{5,6},{6,7},{8,9},{9,10},{10,11},{11... | collective-permute-start | bytes 98312 | tf_op jit(solution)/shard_map/ppermute | solution.py:504
  142.0 5.2 %collective-permute-start.1 = (bf16[2,32,256]{2,1,0:T(8,128)(2,1)S(1)}, bf16[2,32,256]{2,1,0:T(8,128)(2,1)S(1)}, u32[]{:S(2)}, u32[]{:S(2)}) collective-permute-start(bf16[2,32,256]{2,1,0:T(8,128)(2,1)S(1)} %get-tuple-element.14), channel_id=1, source_target_pairs={{1,0},{2,1},{3,2},{4,3},{5,4},{6,5},{7,6},{9,8},{10,9},{11,10},{12... | collective-permute-start | bytes 98312 | tf_op jit(solution)/shard_map/ppermute | solution.py:505

commit v3 on v2

--- a/solution.py
+++ b/solution.py
@@ -272,12 +272,12 @@
     v_at = local_heads * pair
     v_width = local_heads * head_dim
     first = lax.broadcasted_iota(jnp.int32, (BLOCK, pair), 1) < head_dim
-    stacked = []
+    queries = []
     for h in range(local_heads):
         coded = q_ref[:, h * pair : (h + 1) * pair].astype(f32)
         turned = pltpu.roll(coded, head_dim, 1)
         high, low = jnp.where(first, coded, turned), jnp.where(first, turned, coded)
-        stacked.append(jnp.concatenate([high, low], axis=0).astype(bf16))
+        queries.append(jnp.concatenate([high, low], axis=1).astype(bf16))
 
     def chunk(c, carry):
         offsets = []
@@ -293,13 +293,19 @@
         out = []
         for h in range(local_heads):
             top, total, blend = carry[h]
-            scores = []
-            for at, ok in zip(offsets, valid):
-                keys = kv_ref[pl.ds(at, BLOCK), h * pair : (h + 1) * pair]
-                both = lax.dot_general(
-                    stacked[h], keys, (((1,), (1,)), ((), ())), preferred_element_type=f32
-                )
-                scores.append(jnp.where(ok, both[:BLOCK] + both[BLOCK:], -jnp.inf))
+            keys = jnp.concatenate(
+                [kv_ref[pl.ds(at, BLOCK), h * pair : (h + 1) * pair] for at in offsets], axis=0
+            )
+            found = lax.dot_general(
+                queries[h],
+                jnp.concatenate([keys, keys], axis=1),
+                (((1,), (1,)), ((), ())),
+                preferred_element_type=f32,
+            )
+            scores = [
+                jnp.where(ok, found[:, t * BLOCK : (t + 1) * BLOCK], -jnp.inf)
+                for t, ok in enumerate(valid)
+            ]
             peak = functools.reduce(jnp.maximum, scores)
             new_top = jnp.maximum(top, jnp.max(peak, axis=1, keepdims=True))
             scale = jnp.exp(top - new_top)

time: 169 us -> 169 us (level)
  no operation moved by 1% of the time
where the time goes in v3:
time: 169 us
  Pallas kernels  146 us (86%)
  local copies, waits for them, and re-layouts  6.73 us (4%)
  starting transfers between devices  5.97 us (4%)
  matrix products  5.69 us (3%)
  waiting for transfers between devices  2.5 us (1%)
    pallas_call x1, Pallas kernels, exchange(): pl.pallas_call(functools.partial(exchange_kernel, groups, teams), in_spec...  65.2 us
    pallas_call x1, Pallas kernels, attend(): pl.pallas_call(functools.partial(attend_kernel, local_heads, head_dim, sp...  32.1 us
    pallas_call x1, Pallas kernels, predict(): pl.pallas_call(functools.partial(head_kernel, token_rows), grid_spec=pltp...  21.1 us
    pallas_call x1, Pallas kernels, hand_back(): pl.pallas_call(functools.partial(hand_back_kernel, groups), in_specs=[vme...  16.4 us
    pallas_call x1, Pallas kernels, project(): pl.pallas_call(functools.partial(qkv_kernel, local_heads, head_dim), grid...  11.6 us
    unnamed x20, local copies, waits for them, and re-layouts  5.48 us
    dot_general x1, matrix products, on_device(): jnp.dot(attended.astype(f32), out_weight, precision=highest, preferred_el...  4.54 us
    ppermute x1, starting transfers between devices, on_device(): above = lax.ppermute(features[:, strip_tokens - GRID:], 'head', forward)  3.87 us
  transfers between devices with their start and end apart: 2, of which 1 were waited for; matrix products, arithmetic and copies ran while one was open for 0% of the time, Pallas kernels for 0%

profile of v3, /device:TPU:1, one launch (start us, length us, event | category | flops | bytes accessed | tf_op | source)
XLA Modules:
  0.0 169.0 jit_solution(12280504602535377569)
XLA Ops:
  0.0 0.0 copy-start
  0.0 0.0 copy-start.1
  0.0 1.3 copy-done.1
  1.3 0.0 copy-start.7
  1.3 11.6 %qkv.1 = (bf16[2,8,128,256]{3,2,1,0:T(8,128)(2,1)S(1)}, bf16[2,8,128,384]{3,2,1,0:T(8,128)(2,1)S(1)}) custom-call(f32[256,1024]{1,0:T(8,128)S(1)} %bitcast.13, f32[1024,3072]{1,0:T(8,128)} %w_ref.1), custom_call_target="tpu_custom_call" | custom-call | tf_op jit(solution)/shard_map/qkv/pallas_call | solution.py:82
  12.9 0.0 copy-start.4
  12.9 1.1 copy-done.4
  14.1 1.0 copy-done.6
  15.1 65.2 %exchange.1 = (bf16[2,8,128,256]{3,2,1,0:T(8,128)(2,1)}, bf16[8,8,128,384]{3,2,1,0:T(8,128)(2,1)}) custom-call(bf16[2,8,128,256]{3,2,1,0:T(8,128)(2,1)} %copy-done.6, bf16[2,8,128,384]{3,2,1,0:T(8,128)(2,1)} %copy-done.4), custom_call_target="tpu_custom_call" | custom-call | tf_op jit(solution)/shard_map/exchange/pallas_call | solution.py:216
  80.3 0.0 copy-done.7
  80.3 0.0 copy-done.8
  80.3 0.0 copy-start.5
  80.3 1.2 copy-done.5
  81.6 32.1 %attend.1 = bf16[2048,128]{1,0:T(8,128)(2,1)S(1)} custom-call(s32[16,13]{1,0:T(8,128)S(1)} %copy-done.7, s32[16]{0:T(128)S(1)} %copy-done.8, bf16[2048,256]{1,0:T(8,128)(2,1)S(1)} %bitcast.16, bf16[8192,384]{1,0:T(8,128)(2,1)} %bitcast.17), custom_call_target="tpu_custom_call" | custom-call | tf_op jit(solution)/shard_map/attend/pallas_call | solution.py:341
  113.7 0.0 copy-start.3
  113.7 0.8 copy-done.3
  114.5 16.4 %hand_back.1 = bf16[8,2,128,128]{3,2,1,0:T(8,128)(2,1)} custom-call(bf16[2,8,128,128]{3,2,1,0:T(8,128)(2,1)} %bitcast.15), custom_call_target="tpu_custom_call" | custom-call | tf_op jit(solution)/shard_map/hand_back/pallas_call | solution.py:257
  130.8 1.2 copy.11
  132.1 0.0 copy-start.9
  132.1 0.0 copy-done.2
  132.1 4.5 %fusion.7 = (f32[256]{0:T(256)S(1)}, f32[256,1024]{1,0:T(8,128)S(1)}) fusion(f32[256,1024]{1,0:T(8,128)S(1)} %bitcast.14, bf16[256,1024]{0,1:T(8,128)(2,1)S(1)} %bitcast.18, f32[1024,1024]{1,0:T(8,128)} %param.12), kind=kOutput, calls=%fused_computation.14 | convolution fusion | flops 3221749504 | bytes 6816768 | tf_op jit(solution)/shard_map/dot_general | solution.py:499
  136.7 0.3 multiply_reduce_fusion
  136.9 0.0 copy-done
  136.9 0.0 copy-done.9
  136.9 1.2 convolution_convert_fusion
  138.1 3.9 %collective-permute-start = (bf16[2,32,256]{2,1,0:T(8,128)(2,1)S(1)}, bf16[2,32,256]{2,1,0:T(8,128)(2,1)S(1)}, u32[]{:S(2)}, u32[]{:S(2)}) collective-permute-start(bf16[2,32,256]{2,1,0:T(8,128)(2,1)S(1)} %get-tuple-element.13), channel_id=1, source_target_pairs={{0,1},{1,2},{2,3},{3,4},{4,5},{5,6},{6,7},{8,9},{9,10},{10,11},{11... | collective-permute-start | bytes 98312 | tf_op jit(solution)/shard_map/ppermute | solution.py:510
  142.0 2.1 %collective-permute-start.1 = (bf16[2,32,256]{2,1,0:T(8,128)(2,1)S(1)}, bf16[2,32,256]{2,1,0:T(8,128)(2,1)S(1)}, u32[]{:S(2)}, u32[]{:S(2)}) collective-permute-start(bf16[2,32,256]{2,1,0:T(8,128)(2,1)S(1)} %get-tuple-element.14), channel_id=1, source_target_pairs={{1,0},{2,1},{3,2},{4,3},{5,4},{6,5},{7,6},{9,8},{10,9},{11,10},{12... | collective-permute-start | bytes 98312 | tf_op jit(solution)/shard_map/ppermute | solution.py:511
  144.1 0.6 pad_add_fusion.place
  144.7 0.0 collective-permute-done
  144.7 2.5 %collective-permute-done.1 = bf16[2,32,256]{2,1,0:T(8,128)(2,1)S(1)} collective-permute-done((bf16[2,32,256]{2,1,0:T(8,128)(2,1)S(1)}, bf16[2,32,256]{2,1,0:T(8,128)(2,1)S(1)}, u32[]{:S(2)}, u32[]{:S(2)}) %collective-permute-start.1) | collective-permute-done | bytes 32800 | tf_op jit(solution)/shard_map/ppermute | solution.py:511
  147.2 0.7 pad_maximum_fusion.feat_ref
  147.9 21.1 %head.1 = bf16[2,16,128,256]{3,2,1,0:T(8,128)(2,1)} custom-call(s32[2]{0:T(128)} %pad_add_fusion.place, bf16[2,192,256]{2,1,0:T(8,128)(2,1)} %pad_maximum_fusion.feat_ref, bf16[256,4096]{1,0:T(8,128)(2,1)} %up_ref.1, bf16[2,3,3,256,256]{4,3,2,1,0:T(8,128)(2,1)} %conv_ref.1, f32[2,256]{1,0:T(2,128)} %bias_ref.1), custom_call_target="tpu_custom_call" | custom-call | tf_op jit(solution)/shard_map/head/pallas_call | solution.py:441
  (6 shorter events, 0.0 us)
Async XLA Ops:
  0.0 136.9 %copy-start = (f32[1024,256]{1,0:T(8,128)S(1)}, f32[1024,256]{1,0:T(8,128)}, u32[]{:S(2)}) copy-start(f32[1024,256]{1,0:T(8,128)} %param.14) | copy-start | bytes 3145732
  0.0 1.3 copy-start.1
  1.3 79.0 %copy-start.7 = (s32[16,13]{1,0:T(8,128)S(1)}, s32[16,13]{1,0:T(8,128)}, u32[]{:S(2)}) copy-start(s32[16,13]{1,0:T(8,128)} %lists.1) | copy-start | bytes 2500
  1.3 79.0 %copy-start.8 = (s32[16]{0:T(128)S(1)}, s32[16]{0:T(128)}, u32[]{:S(2)}) copy-start(s32[16]{0:T(128)} %counts.1) | copy-start | bytes 196
  12.9 1.1 copy-start.4
  14.1 1.0 copy-start.6
  80.3 1.2 copy-start.5
  81.6 50.6 %copy-start.2 = (f32[2,128,1024]{2,1,0:T(8,128)S(1)}, f32[2,128,1024]{2,1,0:T(8,128)}, u32[]{:S(2)}) copy-start(f32[2,128,1024]{2,1,0:T(8,128)} %param.10) | copy-start | bytes 3145732
  113.7 0.8 copy-start.3
  132.1 4.8 %copy-start.9 = (f32[1024]{0:T(1024)S(1)}, f32[1024]{0:T(1024)}, u32[]{:S(2)}) copy-start(f32[1024]{0:T(1024)} %param.13) | copy-start | bytes 12292
  138.1 6.6 %collective-permute-start = (bf16[2,32,256]{2,1,0:T(8,128)(2,1)S(1)}, bf16[2,32,256]{2,1,0:T(8,128)(2,1)S(1)}, u32[]{:S(2)}, u32[]{:S(2)}) collective-permute-start(bf16[2,32,256]{2,1,0:T(8,128)(2,1)S(1)} %get-tuple-element.13), channel_id=1, source_target_pairs={{0,1},{1,2},{2,3},{3,4},{4,5},{5,6},{6,7},{8,9},{9,10},{10,11},{11... | collective-permute-start | bytes 98312 | tf_op jit(solution)/shard_map/ppermute | solution.py:510
  142.0 5.2 %collective-permute-start.1 = (bf16[2,32,256]{2,1,0:T(8,128)(2,1)S(1)}, bf16[2,32,256]{2,1,0:T(8,128)(2,1)S(1)}, u32[]{:S(2)}, u32[]{:S(2)}) collective-permute-start(bf16[2,32,256]{2,1,0:T(8,128)(2,1)S(1)} %get-tuple-element.14), channel_id=1, source_target_pairs={{1,0},{2,1},{3,2},{4,3},{5,4},{6,5},{7,6},{9,8},{10,9},{11,10},{12... | collective-permute-start | bytes 98312 | tf_op jit(solution)/shard_map/ppermute | solution.py:511
